TPU v7x, 32 devices: a whole 2x2x4 slice. The times are simulated.
32 devices in a mesh: row: 8 (over y, x, core), col: 4 (over z).
Axes of the slice: x: 2, y: 2, z: 4, core: 2. Of those that a mesh axis runs over, the one named last changes fastest.
Arguments:
- tokens: bfloat16 [65536, 1024], P('row', 'col'), may hold values from -6 to 6
- up_weight: bfloat16 [1024, 4096], P('row', 'col'), may hold values from -0.1875 to 0.1875
- hidden_grad: bfloat16 [65536, 4096], P('row', 'col'), may hold values from -6 to 6
Outputs:
- hidden: bfloat16 [65536, 4096], P('row', 'col')
- input_grad: bfloat16 [65536, 1024], P('row', 'col')
All inputs are finite; a program needn't handle non-finite values.
Results may differ from a plain program's by a relative error of at most 0.017.
Values may be sent and summed in bfloat16 or wider, within the bound.
No kernel may reach another device: no remote copies, remote signals or barrier semaphores. Data moves between devices by JAX's collectives and lax.ppermute only.
A program may use at most 128 MiB of HBM per device.

v0:
```python
import jax
import jax.numpy as jnp
from jax import lax
from jax.sharding import PartitionSpec as P

gelu_c = 0.7978845608028654
gelu_a = 0.044715


def gelu_value(v):
    inner = gelu_c * (v + gelu_a * v * v * v)
    return 0.5 * v * (1.0 + jnp.tanh(inner))


def gelu_slope(v):
    inner = gelu_c * (v + gelu_a * v * v * v)
    tval = jnp.tanh(inner)
    return 0.5 * (1.0 + tval) + 0.5 * v * (1.0 - tval * tval) * gelu_c * (
        1.0 + 3.0 * gelu_a * v * v
    )


def per_device(tokens, up_weight, hidden_grad):
    column_panel = lax.all_gather(up_weight, "row", axis=0, tiled=True)
    token_rows = lax.all_gather(tokens, "col", axis=1, tiled=True)
    preact = jnp.dot(token_rows, column_panel, preferred_element_type=jnp.float32)
    hidden = gelu_value(preact).astype(jnp.bfloat16)
    pre_grad = (hidden_grad.astype(jnp.float32) * gelu_slope(preact)).astype(jnp.bfloat16)
    summed = lax.psum_scatter(
        lax.dot_general(
            column_panel, pre_grad, (((1,), (1,)), ((), ())), preferred_element_type=jnp.float32
        ).astype(jnp.bfloat16),
        "col",
        scatter_dimension=0,
        tiled=True,
    ).astype(jnp.float32)
    input_grad = jnp.transpose(summed).astype(jnp.bfloat16)
    return (hidden, input_grad)


def solution(mesh):
    in_specs = (P("row", "col"), P("row", "col"), P("row", "col"))
    out_specs = (P("row", "col"), P("row", "col"))
    return jax.shard_map(
        per_device, mesh=mesh, in_specs=in_specs, out_specs=out_specs, check_vma=False
    )
```

profile of v0, /device:TPU:0, one launch (start us, length us, event | category | flops | bytes accessed | tf_op | source)
XLA Modules:
  0.0 688.1 jit_solution(10581565400900481184)
XLA Ops:
  7.2 0.0 all-gather.5.cloned.1.call-start
  7.2 0.7 all-gather.5.cloned.1.call-update
  7.9 0.0 all-gather.3.cloned.1.call-start
  7.9 0.7 all-gather.3.cloned.1.call-update
  8.6 0.0 reduce-scatter.2.cloned.1.call-start
  8.7 31.7 %all-gather.5.cloned.1.call-done = bf16[1024,1024]{1,0:T(8,128)(2,1)} async-done(((bf16[128,1024]{1,0:T(8,128)(2,1)}), bf16[1024,1024]{1,0:T(8,128)(2,1)}) %all-gather.5.cloned.1.call-update) | async-done | bytes 2097168 | tf_op jit(solution)/shard_map/all_gather | solution.py:24
  40.4 0.0 copy-start
  40.4 287.8 %all-gather.3.cloned.1.call-done = bf16[8192,1024]{1,0:T(8,128)(2,1)} async-done(((bf16[8192,256]{1,0:T(8,128)(2,1)}), bf16[8192,1024]{1,0:T(8,128)(2,1)}) %all-gather.3.cloned.1.call-update) | async-done | bytes 16777232 | tf_op jit(solution)/shard_map/all_gather | solution.py:25
  328.2 34.3 %multiply_convert_fusion = (bf16[8192,1024]{1,0:T(8,128)(2,1)}, f32[8192,1024]{1,0:T(8,128)}) fusion(bf16[8192,1024]{1,0:T(8,128)(2,1)} %all-gather.3.cloned.1.call-done, bf16[1024,1024]{1,0:T(8,128)(2,1)} %all-gather.5.cloned.1.call-done), kind=kOutput, calls=%fused_computation.9 | convolution fusion | flops 17255366656 | bytes 69206016 | tf_op jit(solution)/shard_map/dot_general | solution.py:26
  362.6 0.0 copy-done
  362.6 40.1 %convert_bitcast_fusion = bf16[1024,8192]{0,1:T(8,128)(2,1)} fusion(bf16[1024,1024]{1,0:T(8,128)(2,1)S(1)} %copy-done, f32[8192,1024]{1,0:T(8,128)} %get-tuple-element.3, bf16[8192,1024]{1,0:T(8,128)(2,1)} %param.5), kind=kOutput, calls=%fused_computation.10 | convolution fusion | flops 17356029952 | bytes 69206016 | tf_op jit(solution)/shard_map/dot_general | solution.py:30
  402.7 0.0 reduce-scatter.2.cloned.1.call-update
  402.7 278.8 %reduce-scatter.2.cloned.1.call-done = bf16[256,8192]{0,1:T(8,128)(2,1)} async-done(((bf16[1024,8192]{0,1:T(8,128)(2,1)}), bf16[256,8192]{0,1:T(8,128)(2,1)}) %reduce-scatter.2.cloned.1.call-update) | async-done | bytes 4194320 | tf_op jit(solution)/shard_map/reduce_scatter | solution.py:29
Async XLA Ops:
  7.2 33.2 %all-gather.5.cloned.1.call-start = ((), (), s32[]{:S(2)}) async-start(), calls=%async_computation.2 | async-start | bytes 2359296 | tf_op jit(solution)/shard_map/all_gather | solution.py:24
  7.9 320.3 %all-gather.3.cloned.1.call-start = ((), (), s32[]{:S(2)}) async-start(), calls=%async_computation.1 | async-start | bytes 20971520 | tf_op jit(solution)/shard_map/all_gather | solution.py:25
  8.6 672.9 %reduce-scatter.2.cloned.1.call-start = ((), (), s32[]{:S(2)}) async-start(), calls=%async_computation.3 | async-start | bytes 20971520 | tf_op jit(solution)/shard_map/reduce_scatter | solution.py:29
  40.4 322.2 %copy-start = (bf16[1024,1024]{1,0:T(8,128)(2,1)S(1)}, bf16[1024,1024]{1,0:T(8,128)(2,1)}, u32[]{:S(2)}) copy-start(bf16[1024,1024]{1,0:T(8,128)(2,1)} %all-gather.5.cloned.1.call-done) | copy-start | bytes 6291460
Sparse Core Ops, SparseCore 0:
  9.9 30.4 all-gather.4
  41.9 286.2 all-gather.2
  402.9 278.6 reduce-scatter.1
where the time goes:
time: 688 us
  waiting for transfers between devices  600 us (87%)
  matrix products  74.5 us (11%)
  between operations  13.7 us (2%)
    all_gather x1, waiting for transfers between devices, per_device(): token_rows = lax.all_gather(tokens, 'col', axis=1, tiled=True)  288 us
    reduce_scatter x1, waiting for transfers between devices, per_device(): lax.psum_scatter(lax.dot_general(column_panel, pre_grad, (((1,), (1,)), (...  279 us
    dot_general x1, matrix products, per_device(): lax.dot_general(column_panel, pre_grad, (((1,), (1,)), ((), ())), preferr...  40.1 us
    dot_general x1, matrix products, per_device(): jnp.dot(token_rows, column_panel, preferred_element_type=jnp.float32)  34.3 us
    all_gather x1, waiting for transfers between devices, per_device(): column_panel = lax.all_gather(up_weight, 'row', axis=0, tiled=True)  31.7 us
  transfers between devices with their start and end apart: 3, of which 3 were waited for; matrix products, arithmetic and copies ran while one was open for 0% of the time, Pallas kernels for 0%

commit v1 on v0

--- a/solution.py
+++ b/solution.py
@@ -1,10 +1,16 @@
 import jax
 import jax.numpy as jnp
 from jax import lax
+from jax.experimental import pallas as pl
+from jax.experimental.pallas import tpu as pltpu
 from jax.sharding import PartitionSpec as P
+
 
 gelu_c = 0.7978845608028654
 gelu_a = 0.044715
+
+
+shares = (1, 1, 2, 2, 2, 2, 2, 2, 1, 1)
 
 
 def gelu_value(v):
@@ -20,7 +26,7 @@
     )
 
 
-def per_device(tokens, up_weight, hidden_grad):
+def plain_device(tokens, up_weight, hidden_grad):
     column_panel = lax.all_gather(up_weight, "row", axis=0, tiled=True)
     token_rows = lax.all_gather(tokens, "col", axis=1, tiled=True)
     preact = jnp.dot(token_rows, column_panel, preferred_element_type=jnp.float32)
@@ -38,9 +44,189 @@
     return (hidden, input_grad)
 
 
+def chunk_kernel(place, near_ref, inner_ref, outer_ref, w_ref, wt_ref, grad_ref, *rest):
+    hidden_ref, far_out, near_out = rest[-3:]
+    half = near_ref.shape[1]
+    near_at = pl.multiple_of(place[0] * half, half)
+    far_at = pl.multiple_of((1 - place[0]) * half, half)
+    far = jnp.where(place[1] == 1, inner_ref[...], outer_ref[...])
+    v = jnp.dot(near_ref[...], w_ref[pl.ds(near_at, half), :], preferred_element_type=jnp.float32)
+    v = v + jnp.dot(far, w_ref[pl.ds(far_at, half), :], preferred_element_type=jnp.float32)
+    square = v * v
+    tval = jnp.tanh(gelu_c * (v + gelu_a * square * v))
+    gate = 0.5 * (1.0 + tval)
+    hidden_ref[...] = (v * gate).astype(hidden_ref.dtype)
+    slope = gate + 0.5 * v * (1.0 - tval * tval) * gelu_c * (1.0 + 3.0 * gelu_a * square)
+    pre_grad = (grad_ref[...].astype(jnp.float32) * slope).astype(jnp.bfloat16)
+    far_out[...] = jnp.dot(
+        pre_grad, wt_ref[:, pl.ds(far_at, half)], preferred_element_type=jnp.float32
+    ).astype(far_out.dtype)
+    near_out[...] = jnp.dot(
+        pre_grad, wt_ref[:, pl.ds(near_at, half)], preferred_element_type=jnp.float32
+    ).astype(near_out.dtype)
+
+
+def chunk_call(place, near, inner, outer, w, wt, grad, hidden, row_at):
+    size, half = near.shape
+    rows, width = grad.shape
+    tile = 256 if size % 256 == 0 else size
+    first = row_at // tile
+    features = w.shape[0]
+    args = [place, near, inner, outer, w, wt, grad]
+    in_specs = [
+        pl.BlockSpec((tile, half), lambda i, p: (i, 0)),
+        pl.BlockSpec((tile, half), lambda i, p: (i * p[1], 0)),
+        pl.BlockSpec((tile, half), lambda i, p: (i * (1 - p[1]), 0)),
+        pl.BlockSpec((features, width), lambda i, p: (0, 0)),
+        pl.BlockSpec((width, features), lambda i, p: (0, 0)),
+        pl.BlockSpec((tile, width), lambda i, p: (first + i, 0)),
+    ]
+    aliases = {}
+    if hidden is not None:
+        aliases = {len(args): 0}
+        args.append(hidden)
+        in_specs.append(pl.BlockSpec(memory_space=pl.ANY))
+    return pl.pallas_call(
+        chunk_kernel,
+        grid_spec=pltpu.PrefetchScalarGridSpec(
+            num_scalar_prefetch=1,
+            grid=(size // tile,),
+            in_specs=in_specs,
+            out_specs=[
+                pl.BlockSpec((tile, width), lambda i, p: (first + i, 0)),
+                pl.BlockSpec((tile, half), lambda i, p: (i, 0)),
+                pl.BlockSpec((tile, half), lambda i, p: (i, 0)),
+            ],
+        ),
+        out_shape=[
+            jax.ShapeDtypeStruct((rows, width), jnp.bfloat16),
+            jax.ShapeDtypeStruct((size, half), jnp.bfloat16),
+            jax.ShapeDtypeStruct((size, half), jnp.bfloat16),
+        ],
+        input_output_aliases=aliases,
+        compiler_params=pltpu.CompilerParams(vmem_limit_bytes=40 * 1024 * 1024),
+        cost_estimate=pl.CostEstimate(
+            flops=4 * size * features * width,
+            bytes_accessed=size * (8 * half + 4 * width) + 4 * features * width,
+            transcendentals=size * width,
+        ),
+    )(*args)
+
+
+def panel_kernel(me_ref, block_ref, w_ref, wt_ref):
+    w_ref[...] = block_ref[...]
+    wt_ref[...] = jnp.transpose(block_ref[...])
+
+
+def gather_panel(up_weight, n_row):
+    me = lax.axis_index("row").astype(jnp.int32)
+    block = up_weight
+    bits = n_row.bit_length() - 1
+    for step in range(bits):
+        bit = n_row >> (step + 1)
+        other = lax.ppermute(block, "row", [(i, i ^ bit) for i in range(n_row)])
+        block = jnp.concatenate([block, other], axis=0)
+    depth, width = up_weight.shape
+
+    def place_of(j, p):
+        apart = j ^ p[0]
+        at = 0
+        for step in range(bits):
+            at = at + ((apart >> (bits - 1 - step)) & 1) * (1 << step)
+        return at
+
+    return pl.pallas_call(
+        panel_kernel,
+        grid_spec=pltpu.PrefetchScalarGridSpec(
+            num_scalar_prefetch=1,
+            grid=(n_row,),
+            in_specs=[pl.BlockSpec((depth, width), lambda j, p: (place_of(j, p), 0))],
+            out_specs=[
+                pl.BlockSpec((depth, width), lambda j, p: (j, 0)),
+                pl.BlockSpec((width, depth), lambda j, p: (0, j)),
+            ],
+        ),
+        out_shape=[
+            jax.ShapeDtypeStruct((n_row * depth, width), up_weight.dtype),
+            jax.ShapeDtypeStruct((width, n_row * depth), up_weight.dtype),
+        ],
+        cost_estimate=pl.CostEstimate(
+            flops=0, bytes_accessed=6 * n_row * depth * width, transcendentals=0
+        ),
+    )(me.reshape(1), block)
+
+
+def line_device(n_row, tokens, up_weight, hidden_grad):
+    col = lax.axis_index("col")
+    odd = (col % 2) == 1
+    pair = [(0, 1), (1, 0), (2, 3), (3, 2)]
+    middle = [(1, 2), (2, 1)]
+    outward = [(1, 0), (2, 3)]
+    inward = [(0, 1), (3, 2)]
+
+    def send(x, pairs):
+        return lax.ppermute(x, "col", pairs)
+
+    rows, block = tokens.shape
+    unit = rows // sum(shares)
+    place = jnp.stack([col // 2, ((col == 1) | (col == 2)).astype(jnp.int32)]).astype(jnp.int32)
+
+    w, wt = gather_panel(up_weight, n_row)
+
+    hidden = None
+    input_grad = jnp.zeros((rows, block), jnp.bfloat16)
+    at = 0
+    for share in shares:
+        size = share * unit
+        own = lax.slice_in_dim(tokens, at, at + size, axis=0)
+        partner = send(own, pair)
+        near = jnp.where(
+            odd, jnp.concatenate([partner, own], axis=1), jnp.concatenate([own, partner], axis=1)
+        )
+        inner = send(near, middle)
+        outer = send(inner, outward)
+        hidden, far_part, near_part = chunk_call(
+            place, near, inner, outer, w, wt, hidden_grad, hidden, at
+        )
+        from_end = send(far_part, inward)
+        across = (far_part.astype(jnp.float32) + from_end.astype(jnp.float32)).astype(jnp.bfloat16)
+        from_far = send(across, middle)
+        mine = near_part.astype(jnp.float32) + from_far.astype(jnp.float32)
+        low, high = mine[:, :block], mine[:, block:]
+        for_partner = jnp.where(odd, low, high).astype(jnp.bfloat16)
+        from_partner = send(for_partner, pair)
+        total = (jnp.where(odd, high, low) + from_partner.astype(jnp.float32)).astype(jnp.bfloat16)
+        input_grad = lax.dynamic_update_slice(input_grad, total, (at, 0))
+        at += size
+    return (hidden, input_grad)
+
+
+def fits_line(mesh, tokens, up_weight):
+    n_row, n_col = mesh.shape["row"], mesh.shape["col"]
+    rows, block = tokens.shape[0] // n_row, tokens.shape[1] // n_col
+    return (
+        n_col == 4
+        and n_row & (n_row - 1) == 0
+        and rows % (16 * sum(shares)) == 0
+        and block % 128 == 0
+        and up_weight.shape[1] % (128 * n_col) == 0
+    )
+
+
 def solution(mesh):
-    in_specs = (P("row", "col"), P("row", "col"), P("row", "col"))
-    out_specs = (P("row", "col"), P("row", "col"))
-    return jax.shard_map(
-        per_device, mesh=mesh, in_specs=in_specs, out_specs=out_specs, check_vma=False
-    )
+    specs = (P("row", "col"), P("row", "col"), P("row", "col"))
+
+    def line_body(*blocks):
+        return line_device(mesh.shape["row"], *blocks)
+
+    def mapped(body):
+        return jax.shard_map(body, mesh=mesh, in_specs=specs, out_specs=specs[:2], check_vma=False)
+
+    ordered = mapped(line_body)
+
+    def whole(tokens, up_weight, hidden_grad):
+        if fits_line(mesh, tokens, up_weight):
+            return ordered(tokens, up_weight, hidden_grad)
+        return mapped(plain_device)(tokens, up_weight, hidden_grad)
+
+    return whole

time: 688 us -> 661 us (0.961)
  waiting for transfers between devices: 600 us -> 323 us
  starting transfers between devices: 0.11 us -> 200 us
  Pallas kernels: 0 us -> 87.1 us
  matrix products: 74.5 us -> 0 us
  other arithmetic: 0 us -> 31.8 us
  local copies, waits for them, and re-layouts: 0.01 us -> 16.3 us
  between operations: 13.7 us -> 1.62 us
    ppermute x0 -> x63, waiting for transfers between devices: none -> 323 us  [the longest x60 321 us: send(): return lax.ppermute(x, 'col', pairs)]
    all_gather x2 -> x0, waiting for transfers between devices: 320 us -> none  [the longest x1 288 us: per_device(): token_rows = lax.all_gather(tokens, 'col', axis=1, tiled=True)]
    reduce_scatter x1 -> x0, waiting for transfers between devices: 279 us -> none  [per_device(): lax.psum_scatter(lax.dot_general(column_panel, pre_grad, (((1,), (1,)), (...]
    ppermute x0 -> x63, starting transfers between devices: none -> 200 us  [the longest x60 195 us: send(): return lax.ppermute(x, 'col', pairs)]
    pallas_call x0 -> x11, Pallas kernels: none -> 87.1 us  [the longest x10 80.9 us: chunk_call(): pl.pallas_call(chunk_kernel, grid_spec=pltpu.PrefetchScalarGridSpec(num_s...]
    dot_general x2 -> x0, matrix products: 74.5 us -> none  [the longest x1 40.1 us: per_device(): lax.dot_general(column_panel, pre_grad, (((1,), (1,)), ((), ())), preferr...]
    select_n x0 -> x10, other arithmetic: none -> 15.9 us  [line_device(): jnp.where(odd, jnp.concatenate([partner, own], axis=1), jnp.concatenate([...]
    unnamed x2 -> x72, local copies, waits for them, and re-layouts: 0.01 us -> 11.7 us
  transfers between devices with their start and end apart: 3 -> 63, of which waited for: 3 -> 28; matrix products, arithmetic and copies ran while one was open for 0% -> 6% of each run, Pallas kernels for 0% -> 13%
where the time goes in v1:
time: 661 us; the launch traced here: 659 us
  waiting for transfers between devices  323 us (49%)
  starting transfers between devices  200 us (30%)
  Pallas kernels  87.1 us (13%)
  other arithmetic  31.8 us (5%)
  local copies, waits for them, and re-layouts  16.3 us (2%)
    ppermute x60, waiting for transfers between devices, send(): return lax.ppermute(x, 'col', pairs)  321 us
    ppermute x60, starting transfers between devices, send(): return lax.ppermute(x, 'col', pairs)  195 us
    pallas_call x10, Pallas kernels, chunk_call(): pl.pallas_call(chunk_kernel, grid_spec=pltpu.PrefetchScalarGridSpec(num_s...  80.9 us
    select_n x10, other arithmetic, line_device(): jnp.where(odd, jnp.concatenate([partner, own], axis=1), jnp.concatenate([...  15.9 us
  transfers between devices with their start and end apart: 63, of which 28 were waited for; matrix products, arithmetic and copies ran while one was open for 6% of the time, Pallas kernels for 13%

profile of v1, /device:TPU:0, one launch (start us, length us, event | category | flops | bytes accessed | tf_op | source)
XLA Modules:
  0.0 659.4 jit_solution(7036454476096637459)
XLA Ops:
  29.1 13.4 %collective-permute-done = bf16[512,256]{1,0:T(8,128)(2,1)} collective-permute-done((bf16[512,256]{1,0:T(8,128)(2,1)S(1)}, bf16[512,256]{1,0:T(8,128)(2,1)}, u32[]{:S(2)}, u32[]{:S(2)}) %collective-permute-start) | collective-permute-done | bytes 262176 | tf_op jit(solution)/shard_map/ppermute | solution.py:168
  55.2 9.7 %collective-permute-done.18 = bf16[1024,256]{1,0:T(8,128)(2,1)} collective-permute-done((bf16[1024,256]{1,0:T(8,128)(2,1)S(1)}, bf16[1024,256]{1,0:T(8,128)(2,1)}, u32[]{:S(2)}, u32[]{:S(2)}) %collective-permute-start.18) | collective-permute-done | bytes 524320 | tf_op jit(solution)/shard_map/ppermute | solution.py:168
  89.0 9.6 %collective-permute-done.9 = bf16[1024,256]{1,0:T(8,128)(2,1)} collective-permute-done((bf16[1024,256]{1,0:T(8,128)(2,1)}, bf16[1024,256]{1,0:T(8,128)(2,1)}, u32[]{:S(2)}, u32[]{:S(2)}) %collective-permute-start.9) | collective-permute-done | bytes 524320 | tf_op jit(solution)/shard_map/ppermute | solution.py:168
  141.2 34.1 %collective-permute-start.36 = (bf16[512,512]{1,0:T(8,128)(2,1)S(1)}, bf16[512,512]{1,0:T(8,128)(2,1)S(1)}, u32[]{:S(2)}, u32[]{:S(2)}) collective-permute-start(bf16[512,512]{1,0:T(8,128)(2,1)S(1)} %get-tuple-element.49), channel_id=1, source_target_pairs={{0,1},{3,2},{4,5},{7,6},{8,9},{11,10},{12,13},{15,14},{16,17},{19,... | collective-permute-start | bytes 1572872 | tf_op jit(solution)/shard_map/ppermute | solution.py:168
  196.7 9.3 %collective-permute-done.26.outer_ref = bf16[1024,512]{1,0:T(8,128)(2,1)S(1)} collective-permute-done((bf16[1024,512]{1,0:T(8,128)(2,1)}, bf16[1024,512]{1,0:T(8,128)(2,1)S(1)}, u32[]{:S(2)}, u32[]{:S(2)}) %collective-permute-start.26) | collective-permute-done | bytes 1048608 | tf_op jit(solution)/shard_map/ppermute | solution.py:168
  207.3 9.7 %shard_map.53 = (bf16[8192,1024]{1,0:T(8,128)(2,1)}, bf16[1024,512]{1,0:T(8,128)(2,1)S(1)}, bf16[1024,512]{1,0:T(8,128)(2,1)S(1)}) custom-call(s32[2]{0:T(128)S(1)} %pad_add_fusion.place, bf16[1024,512]{1,0:T(8,128)(2,1)} %maximum_select_fusion.5.near_ref, bf16[1024,512]{1,0:T(8,128)(2,1)} %collective-permute-done.25.inner_ref, ...), custom_call_target="tpu_custom_call", output_to_operand_aliasing={{0}: (7, {})} | custom-call | flops 4294967296 | bytes 12582912 | tf_op jit(solution)/shard_map/pallas_call | solution.py:89
  217.0 11.4 %collective-permute-done.23.outer_ref = bf16[1024,512]{1,0:T(8,128)(2,1)S(1)} collective-permute-done((bf16[1024,512]{1,0:T(8,128)(2,1)}, bf16[1024,512]{1,0:T(8,128)(2,1)S(1)}, u32[]{:S(2)}, u32[]{:S(2)}) %collective-permute-start.23) | collective-permute-done | bytes 1048608 | tf_op jit(solution)/shard_map/ppermute | solution.py:168
  229.9 9.4 %shard_map.54 = (bf16[8192,1024]{1,0:T(8,128)(2,1)}, bf16[1024,512]{1,0:T(8,128)(2,1)S(1)}, bf16[1024,512]{1,0:T(8,128)(2,1)S(1)}) custom-call(s32[2]{0:T(128)S(1)} %pad_add_fusion.place, bf16[1024,512]{1,0:T(8,128)(2,1)S(1)} %maximum_select_fusion.4.near_ref, bf16[1024,512]{1,0:T(8,128)(2,1)} %collective-permute-done.22.inner_ref, ...), custom_call_target="tpu_custom_call", output_to_operand_aliasing={{0}: (7, {})} | custom-call | flops 4294967296 | bytes 12582912 | tf_op jit(solution)/shard_map/pallas_call | solution.py:89
  241.9 9.0 %collective-permute-done.20.outer_ref = bf16[1024,512]{1,0:T(8,128)(2,1)S(1)} collective-permute-done((bf16[1024,512]{1,0:T(8,128)(2,1)}, bf16[1024,512]{1,0:T(8,128)(2,1)S(1)}, u32[]{:S(2)}, u32[]{:S(2)}) %collective-permute-start.20) | collective-permute-done | bytes 1048608 | tf_op jit(solution)/shard_map/ppermute | solution.py:168
  252.2 9.4 %shard_map.55 = (bf16[8192,1024]{1,0:T(8,128)(2,1)}, bf16[1024,512]{1,0:T(8,128)(2,1)S(1)}, bf16[1024,512]{1,0:T(8,128)(2,1)S(1)}) custom-call(s32[2]{0:T(128)S(1)} %pad_add_fusion.place, bf16[1024,512]{1,0:T(8,128)(2,1)S(1)} %maximum_select_fusion.3.near_ref, bf16[1024,512]{1,0:T(8,128)(2,1)} %collective-permute-done.19.inner_ref, ...), custom_call_target="tpu_custom_call", output_to_operand_aliasing={{0}: (7, {})} | custom-call | flops 4294967296 | bytes 12582912 | tf_op jit(solution)/shard_map/pallas_call | solution.py:89
  261.6 11.8 %collective-permute-done.17.outer_ref = bf16[1024,512]{1,0:T(8,128)(2,1)S(1)} collective-permute-done((bf16[1024,512]{1,0:T(8,128)(2,1)S(1)}, bf16[1024,512]{1,0:T(8,128)(2,1)S(1)}, u32[]{:S(2)}, u32[]{:S(2)}) %collective-permute-start.17) | collective-permute-done | bytes 1048608 | tf_op jit(solution)/shard_map/ppermute | solution.py:168
  274.9 9.5 %shard_map.56 = (bf16[8192,1024]{1,0:T(8,128)(2,1)}, bf16[1024,512]{1,0:T(8,128)(2,1)S(1)}, bf16[1024,512]{1,0:T(8,128)(2,1)S(1)}) custom-call(s32[2]{0:T(128)S(1)} %pad_add_fusion.place, bf16[1024,512]{1,0:T(8,128)(2,1)S(1)} %maximum_select_fusion.2.near_ref, ...), custom_call_target="tpu_custom_call", output_to_operand_aliasing={{0}: (7, {})} | custom-call | flops 4294967296 | bytes 12582912 | tf_op jit(solution)/shard_map/pallas_call | solution.py:89
  285.4 10.5 %collective-permute-done.14.outer_ref = bf16[1024,512]{1,0:T(8,128)(2,1)S(1)} collective-permute-done((bf16[1024,512]{1,0:T(8,128)(2,1)S(1)}, bf16[1024,512]{1,0:T(8,128)(2,1)S(1)}, u32[]{:S(2)}, u32[]{:S(2)}) %collective-permute-start.14) | collective-permute-done | bytes 1048608 | tf_op jit(solution)/shard_map/ppermute | solution.py:168
  296.6 9.6 %shard_map.57 = (bf16[8192,1024]{1,0:T(8,128)(2,1)}, bf16[1024,512]{1,0:T(8,128)(2,1)S(1)}, bf16[1024,512]{1,0:T(8,128)(2,1)S(1)}) custom-call(s32[2]{0:T(128)S(1)} %pad_add_fusion.place, bf16[1024,512]{1,0:T(8,128)(2,1)S(1)} %maximum_select_fusion.1.near_ref, ...), custom_call_target="tpu_custom_call", output_to_operand_aliasing={{0}: (7, {})} | custom-call | flops 4294967296 | bytes 12582912 | tf_op jit(solution)/shard_map/pallas_call | solution.py:89
  306.1 26.2 %collective-permute-done.11.outer_ref = bf16[1024,512]{1,0:T(8,128)(2,1)S(1)} collective-permute-done((bf16[1024,512]{1,0:T(8,128)(2,1)S(1)}, bf16[1024,512]{1,0:T(8,128)(2,1)S(1)}, u32[]{:S(2)}, u32[]{:S(2)}) %collective-permute-start.11) | collective-permute-done | bytes 1048608 | tf_op jit(solution)/shard_map/ppermute | solution.py:168
  332.3 9.6 %shard_map.58 = (bf16[8192,1024]{1,0:T(8,128)(2,1)}, bf16[1024,512]{1,0:T(8,128)(2,1)S(1)}, bf16[1024,512]{1,0:T(8,128)(2,1)S(1)}) custom-call(s32[2]{0:T(128)S(1)} %pad_add_fusion.place, bf16[1024,512]{1,0:T(8,128)(2,1)S(1)} %maximum_select_fusion.near_ref, ...), custom_call_target="tpu_custom_call", output_to_operand_aliasing={{0}: (7, {})} | custom-call | flops 4294967296 | bytes 12582912 | tf_op jit(solution)/shard_map/pallas_call | solution.py:89
  370.5 75.2 %collective-permute-done.35 = bf16[512,256]{1,0:T(8,128)(2,1)S(1)} collective-permute-done((bf16[512,256]{1,0:T(8,128)(2,1)S(1)}, bf16[512,256]{1,0:T(8,128)(2,1)S(1)}, u32[]{:S(2)}, u32[]{:S(2)}) %collective-permute-start.35) | collective-permute-done | bytes 262176 | tf_op jit(solution)/shard_map/ppermute | solution.py:168
  469.6 17.1 %collective-permute-done.45 = bf16[1024,512]{1,0:T(8,128)(2,1)S(1)} collective-permute-done((bf16[1024,512]{1,0:T(8,128)(2,1)S(1)}, bf16[1024,512]{1,0:T(8,128)(2,1)S(1)}, u32[]{:S(2)}, u32[]{:S(2)}) %collective-permute-start.45) | collective-permute-done | bytes 1048608 | tf_op jit(solution)/shard_map/ppermute | solution.py:168
  488.7 20.5 %collective-permute-done.42 = bf16[1024,512]{1,0:T(8,128)(2,1)S(1)} collective-permute-done((bf16[1024,512]{1,0:T(8,128)(2,1)S(1)}, bf16[1024,512]{1,0:T(8,128)(2,1)S(1)}, u32[]{:S(2)}, u32[]{:S(2)}) %collective-permute-start.42) | collective-permute-done | bytes 1048608 | tf_op jit(solution)/shard_map/ppermute | solution.py:168
  512.0 14.1 %collective-permute-done.39 = bf16[1024,512]{1,0:T(8,128)(2,1)S(1)} collective-permute-done((bf16[1024,512]{1,0:T(8,128)(2,1)S(1)}, bf16[1024,512]{1,0:T(8,128)(2,1)S(1)}, u32[]{:S(2)}, u32[]{:S(2)}) %collective-permute-start.39) | collective-permute-done | bytes 1048608 | tf_op jit(solution)/shard_map/ppermute | solution.py:168
  530.6 69.8 %collective-permute-start.56 = (bf16[1024,256]{1,0:T(8,128)(2,1)S(1)}, bf16[1024,256]{1,0:T(8,128)(2,1)S(1)}, u32[]{:S(2)}, u32[]{:S(2)}) collective-permute-start(bf16[1024,256]{1,0:T(8,128)(2,1)S(1)} %select_convert_fusion), channel_id=1, source_target_pairs={{0,1},{1,0},{2,3},{3,2},{4,5},{5,4},{6,7},{7,6},{8,9},{9,8},{10,11... | collective-permute-start | bytes 1572872 | tf_op jit(solution)/shard_map/ppermute | solution.py:168
  602.0 9.7 %collective-permute-start.41 = (bf16[1024,256]{1,0:T(8,128)(2,1)S(1)}, bf16[1024,256]{1,0:T(8,128)(2,1)S(1)}, u32[]{:S(2)}, u32[]{:S(2)}) collective-permute-start(bf16[1024,256]{1,0:T(8,128)(2,1)S(1)} %select_convert_fusion.5), channel_id=1, source_target_pairs={{0,1},{1,0},{2,3},{3,2},{4,5},{5,4},{6,7},{7,6},{8,9},{9,8},{10,11... | collective-permute-start | bytes 1572872 | tf_op jit(solution)/shard_map/ppermute | solution.py:168
  612.3 20.8 %collective-permute-done.41 = bf16[1024,256]{1,0:T(8,128)(2,1)S(1)} collective-permute-done((bf16[1024,256]{1,0:T(8,128)(2,1)S(1)}, bf16[1024,256]{1,0:T(8,128)(2,1)S(1)}, u32[]{:S(2)}, u32[]{:S(2)}) %collective-permute-start.41) | collective-permute-done | bytes 524320 | tf_op jit(solution)/shard_map/ppermute | solution.py:168
  635.7 9.8 %collective-permute-done.47 = bf16[1024,256]{1,0:T(8,128)(2,1)S(1)} collective-permute-done((bf16[1024,256]{1,0:T(8,128)(2,1)S(1)}, bf16[1024,256]{1,0:T(8,128)(2,1)S(1)}, u32[]{:S(2)}, u32[]{:S(2)}) %collective-permute-start.47) | collective-permute-done | bytes 524320 | tf_op jit(solution)/shard_map/ppermute | solution.py:168
  (242 shorter events, 218.6 us)
Async XLA Ops:
  46.8 65.2 %collective-permute-start.5 = (bf16[512,1024]{1,0:T(8,128)(2,1)}, bf16[512,1024]{1,0:T(8,128)(2,1)}, u32[]{:S(2)}, u32[]{:S(2)}) collective-permute-start(bf16[512,1024]{1,0:T(8,128)(2,1)} %pad_maximum_fusion.1), channel_id=1, source_target_pairs={{0,4},{4,0},{8,12},{12,8},{16,20},{20,16},{24,28},{28,24},{1,5},{5... | collective-permute-start | bytes 3145736 | tf_op jit(solution)/shard_map/ppermute | solution.py:127
  87.4 89.7 %collective-permute-start.25 = (bf16[1024,512]{1,0:T(8,128)(2,1)}, bf16[1024,512]{1,0:T(8,128)(2,1)}, u32[]{:S(2)}, u32[]{:S(2)}) collective-permute-start(bf16[1024,512]{1,0:T(8,128)(2,1)} %maximum_select_fusion.5.near_ref), channel_id=1, source_target_pairs={{1,2},{2,1},{5,6},{6,5},{9,10},{10,9},{13,14},{14,13},{17,18},{18,... | collective-permute-start | bytes 3145736 | tf_op jit(solution)/shard_map/ppermute | solution.py:168
  98.6 79.3 %collective-permute-start.22 = (bf16[1024,512]{1,0:T(8,128)(2,1)S(1)}, bf16[1024,512]{1,0:T(8,128)(2,1)}, u32[]{:S(2)}, u32[]{:S(2)}) collective-permute-start(bf16[1024,512]{1,0:T(8,128)(2,1)S(1)} %maximum_select_fusion.4.near_ref), channel_id=1, source_target_pairs={{1,2},{2,1},{5,6},{6,5},{9,10},{10,9},{13,14},{14,13},{17,18},{18,... | collective-permute-start | bytes 3145736 | tf_op jit(solution)/shard_map/ppermute | solution.py:168
  102.8 76.4 %collective-permute-start.19 = (bf16[1024,512]{1,0:T(8,128)(2,1)S(1)}, bf16[1024,512]{1,0:T(8,128)(2,1)}, u32[]{:S(2)}, u32[]{:S(2)}) collective-permute-start(bf16[1024,512]{1,0:T(8,128)(2,1)S(1)} %maximum_select_fusion.3.near_ref), channel_id=1, source_target_pairs={{1,2},{2,1},{5,6},{6,5},{9,10},{10,9},{13,14},{14,13},{17,18},{18,... | collective-permute-start | bytes 3145736 | tf_op jit(solution)/shard_map/ppermute | solution.py:168
  134.4 57.1 %collective-permute-start.16 = (bf16[1024,512]{1,0:T(8,128)(2,1)S(1)}, bf16[1024,512]{1,0:T(8,128)(2,1)S(1)}, u32[]{:S(2)}, u32[]{:S(2)}) collective-permute-start(bf16[1024,512]{1,0:T(8,128)(2,1)S(1)} %maximum_select_fusion.2.near_ref), channel_id=1, source_target_pairs={{1,2},{2,1},{5,6},{6,5},{9,10},{10,9},{13,14},{14,13},{17,18},{18,... | collective-permute-start | bytes 3145736 | tf_op jit(solution)/shard_map/ppermute | solution.py:168
  192.9 58.0 %collective-permute-start.20 = (bf16[1024,512]{1,0:T(8,128)(2,1)}, bf16[1024,512]{1,0:T(8,128)(2,1)S(1)}, u32[]{:S(2)}, u32[]{:S(2)}) collective-permute-start(bf16[1024,512]{1,0:T(8,128)(2,1)} %collective-permute-done.19.inner_ref), channel_id=1, source_target_pairs={{1,0},{2,3},{5,4},{6,7},{9,8},{10,11},{13,12},{14,15},{17,16},{18,... | collective-permute-start | bytes 3145736 | tf_op jit(solution)/shard_map/ppermute | solution.py:168
  206.0 67.4 %collective-permute-start.17 = (bf16[1024,512]{1,0:T(8,128)(2,1)S(1)}, bf16[1024,512]{1,0:T(8,128)(2,1)S(1)}, u32[]{:S(2)}, u32[]{:S(2)}) collective-permute-start(bf16[1024,512]{1,0:T(8,128)(2,1)S(1)} %collective-permute-done.16.inner_ref), channel_id=1, source_target_pairs={{1,0},{2,3},{5,4},{6,7},{9,8},{10,11},{13,12},{14,15},{17,16},{18,... | collective-permute-start | bytes 3145736 | tf_op jit(solution)/shard_map/ppermute | solution.py:168
  228.5 67.4 %collective-permute-start.14 = (bf16[1024,512]{1,0:T(8,128)(2,1)S(1)}, bf16[1024,512]{1,0:T(8,128)(2,1)S(1)}, u32[]{:S(2)}, u32[]{:S(2)}) collective-permute-start(bf16[1024,512]{1,0:T(8,128)(2,1)S(1)} %collective-permute-done.13.inner_ref), channel_id=1, source_target_pairs={{1,0},{2,3},{5,4},{6,7},{9,8},{10,11},{13,12},{14,15},{17,16},{18,... | collective-permute-start | bytes 3145736 | tf_op jit(solution)/shard_map/ppermute | solution.py:168
  239.3 102.6 %collective-permute-start.8 = (bf16[512,512]{1,0:T(8,128)(2,1)}, bf16[512,512]{1,0:T(8,128)(2,1)}, u32[]{:S(2)}, u32[]{:S(2)}) collective-permute-start(bf16[512,512]{1,0:T(8,128)(2,1)} %collective-permute-done.7.inner_ref), channel_id=1, source_target_pairs={{1,0},{2,3},{5,4},{6,7},{9,8},{10,11},{13,12},{14,15},{17,16},{18,... | collective-permute-start | bytes 1572872 | tf_op jit(solution)/shard_map/ppermute | solution.py:168
  240.6 107.4 %collective-permute-start.2 = (bf16[512,512]{1,0:T(8,128)(2,1)}, bf16[512,512]{1,0:T(8,128)(2,1)}, u32[]{:S(2)}, u32[]{:S(2)}) collective-permute-start(bf16[512,512]{1,0:T(8,128)(2,1)} %collective-permute-done.1.inner_ref), channel_id=1, source_target_pairs={{1,0},{2,3},{5,4},{6,7},{9,8},{10,11},{13,12},{14,15},{17,16},{18,... | collective-permute-start | bytes 1572872 | tf_op jit(solution)/shard_map/ppermute | solution.py:168
  250.9 81.4 %collective-permute-start.11 = (bf16[1024,512]{1,0:T(8,128)(2,1)S(1)}, bf16[1024,512]{1,0:T(8,128)(2,1)S(1)}, u32[]{:S(2)}, u32[]{:S(2)}) collective-permute-start(bf16[1024,512]{1,0:T(8,128)(2,1)S(1)} %collective-permute-done.10.inner_ref), channel_id=1, source_target_pairs={{1,0},{2,3},{5,4},{6,7},{9,8},{10,11},{13,12},{14,15},{17,16},{18,... | collective-permute-start | bytes 3145736 | tf_op jit(solution)/shard_map/ppermute | solution.py:168
  273.4 84.9 %collective-permute-start.37 = (bf16[512,512]{1,0:T(8,128)(2,1)}, bf16[512,512]{1,0:T(8,128)(2,1)}, u32[]{:S(2)}, u32[]{:S(2)}) collective-permute-start(bf16[512,512]{1,0:T(8,128)(2,1)} %add_convert_fusion.14), channel_id=1, source_target_pairs={{1,2},{2,1},{5,6},{6,5},{9,10},{10,9},{13,14},{14,13},{17,18},{18,... | collective-permute-start | bytes 1572872 | tf_op jit(solution)/shard_map/ppermute | solution.py:168
  295.9 65.1 %collective-permute-start.34 = (bf16[512,512]{1,0:T(8,128)(2,1)}, bf16[512,512]{1,0:T(8,128)(2,1)S(1)}, u32[]{:S(2)}, u32[]{:S(2)}) collective-permute-start(bf16[512,512]{1,0:T(8,128)(2,1)} %add_convert_fusion.15), channel_id=1, source_target_pairs={{1,2},{2,1},{5,6},{6,5},{9,10},{10,9},{13,14},{14,13},{17,18},{18,... | collective-permute-start | bytes 1572872 | tf_op jit(solution)/shard_map/ppermute | solution.py:168
  355.7 91.2 %collective-permute-start.57 = (bf16[512,512]{1,0:T(8,128)(2,1)S(1)}, bf16[512,512]{1,0:T(8,128)(2,1)S(1)}, u32[]{:S(2)}, u32[]{:S(2)}) collective-permute-start(bf16[512,512]{1,0:T(8,128)(2,1)S(1)} %get-tuple-element.63), channel_id=1, source_target_pairs={{0,1},{3,2},{4,5},{7,6},{8,9},{11,10},{12,13},{15,14},{16,17},{19,... | collective-permute-start | bytes 1572872 | tf_op jit(solution)/shard_map/ppermute | solution.py:168
  357.0 107.9 %collective-permute-start.54 = (bf16[1024,512]{1,0:T(8,128)(2,1)S(1)}, bf16[1024,512]{1,0:T(8,128)(2,1)S(1)}, u32[]{:S(2)}, u32[]{:S(2)}) collective-permute-start(bf16[1024,512]{1,0:T(8,128)(2,1)S(1)} %get-tuple-element.61), channel_id=1, source_target_pairs={{0,1},{3,2},{4,5},{7,6},{8,9},{11,10},{12,13},{15,14},{16,17},{19,... | collective-permute-start | bytes 3145736 | tf_op jit(solution)/shard_map/ppermute | solution.py:168
  358.4 108.3 %collective-permute-start.51 = (bf16[1024,512]{1,0:T(8,128)(2,1)S(1)}, bf16[1024,512]{1,0:T(8,128)(2,1)S(1)}, u32[]{:S(2)}, u32[]{:S(2)}) collective-permute-start(bf16[1024,512]{1,0:T(8,128)(2,1)S(1)} %get-tuple-element.59), channel_id=1, source_target_pairs={{0,1},{3,2},{4,5},{7,6},{8,9},{11,10},{12,13},{15,14},{16,17},{19,... | collective-permute-start | bytes 3145736 | tf_op jit(solution)/shard_map/ppermute | solution.py:168
  361.0 106.7 %collective-permute-start.48 = (bf16[1024,512]{1,0:T(8,128)(2,1)S(1)}, bf16[1024,512]{1,0:T(8,128)(2,1)S(1)}, u32[]{:S(2)}, u32[]{:S(2)}) collective-permute-start(bf16[1024,512]{1,0:T(8,128)(2,1)S(1)} %get-tuple-element.57), channel_id=1, source_target_pairs={{0,1},{3,2},{4,5},{7,6},{8,9},{11,10},{12,13},{15,14},{16,17},{19,... | collective-permute-start | bytes 3145736 | tf_op jit(solution)/shard_map/ppermute | solution.py:168
  367.9 77.9 %collective-permute-start.35 = (bf16[512,256]{1,0:T(8,128)(2,1)S(1)}, bf16[512,256]{1,0:T(8,128)(2,1)S(1)}, u32[]{:S(2)}, u32[]{:S(2)}) collective-permute-start(bf16[512,256]{1,0:T(8,128)(2,1)S(1)} %select_convert_fusion.9), channel_id=1, source_target_pairs={{0,1},{1,0},{2,3},{3,2},{4,5},{5,4},{6,7},{7,6},{8,9},{9,8},{10,11... | collective-permute-start | bytes 786440 | tf_op jit(solution)/shard_map/ppermute | solution.py:168
  464.9 61.1 %collective-permute-start.39 = (bf16[1024,512]{1,0:T(8,128)(2,1)S(1)}, bf16[1024,512]{1,0:T(8,128)(2,1)S(1)}, u32[]{:S(2)}, u32[]{:S(2)}) collective-permute-start(bf16[1024,512]{1,0:T(8,128)(2,1)S(1)} %get-tuple-element.51), channel_id=1, source_target_pairs={{0,1},{3,2},{4,5},{7,6},{8,9},{11,10},{12,13},{15,14},{16,17},{19,... | collective-permute-start | bytes 3145736 | tf_op jit(solution)/shard_map/ppermute | solution.py:168
  467.7 189.6 %collective-permute-start.62 = (bf16[512,256]{1,0:T(8,128)(2,1)S(1)}, bf16[512,256]{1,0:T(8,128)(2,1)S(1)}, u32[]{:S(2)}, u32[]{:S(2)}) collective-permute-start(bf16[512,256]{1,0:T(8,128)(2,1)S(1)} %select_convert_fusion.6), channel_id=1, source_target_pairs={{0,1},{1,0},{2,3},{3,2},{4,5},{5,4},{6,7},{7,6},{8,9},{9,8},{10,11... | collective-permute-start | bytes 786440 | tf_op jit(solution)/shard_map/ppermute | solution.py:168
  509.2 148.0 %collective-permute-start.59 = (bf16[512,256]{1,0:T(8,128)(2,1)S(1)}, bf16[512,256]{1,0:T(8,128)(2,1)S(1)}, u32[]{:S(2)}, u32[]{:S(2)}) collective-permute-start(bf16[512,256]{1,0:T(8,128)(2,1)S(1)} %select_convert_fusion.7), channel_id=1, source_target_pairs={{0,1},{1,0},{2,3},{3,2},{4,5},{5,4},{6,7},{7,6},{8,9},{9,8},{10,11... | collective-permute-start | bytes 786440 | tf_op jit(solution)/shard_map/ppermute | solution.py:168
  527.1 73.8 %collective-permute-start.49 = (bf16[1024,512]{1,0:T(8,128)(2,1)S(1)}, bf16[1024,512]{1,0:T(8,128)(2,1)S(1)}, u32[]{:S(2)}, u32[]{:S(2)}) collective-permute-start(bf16[1024,512]{1,0:T(8,128)(2,1)S(1)} %add_convert_fusion.2), channel_id=1, source_target_pairs={{1,2},{2,1},{5,6},{6,5},{9,10},{10,9},{13,14},{14,13},{17,18},{18,... | collective-permute-start | bytes 3145736 | tf_op jit(solution)/shard_map/ppermute | solution.py:168
  529.3 72.7 %collective-permute-start.46 = (bf16[1024,512]{1,0:T(8,128)(2,1)S(1)}, bf16[1024,512]{1,0:T(8,128)(2,1)S(1)}, u32[]{:S(2)}, u32[]{:S(2)}) collective-permute-start(bf16[1024,512]{1,0:T(8,128)(2,1)S(1)} %add_convert_fusion.3), channel_id=1, source_target_pairs={{1,2},{2,1},{5,6},{6,5},{9,10},{10,9},{13,14},{14,13},{17,18},{18,... | collective-permute-start | bytes 3145736 | tf_op jit(solution)/shard_map/ppermute | solution.py:168
  530.6 126.3 %collective-permute-start.56 = (bf16[1024,256]{1,0:T(8,128)(2,1)S(1)}, bf16[1024,256]{1,0:T(8,128)(2,1)S(1)}, u32[]{:S(2)}, u32[]{:S(2)}) collective-permute-start(bf16[1024,256]{1,0:T(8,128)(2,1)S(1)} %select_convert_fusion), channel_id=1, source_target_pairs={{0,1},{1,0},{2,3},{3,2},{4,5},{5,4},{6,7},{7,6},{8,9},{9,8},{10,11... | collective-permute-start | bytes 1572872 | tf_op jit(solution)/shard_map/ppermute | solution.py:168
  (75 other events, 1686.6 us)

commit v2 on v0

--- a/solution.py
+++ b/solution.py
@@ -1,10 +1,20 @@
+import functools
+
 import jax
 import jax.numpy as jnp
 from jax import lax
+from jax.experimental import pallas as pl
+from jax.experimental.pallas import tpu as pltpu
 from jax.sharding import PartitionSpec as P
+
 
 gelu_c = 0.7978845608028654
 gelu_a = 0.044715
+
+
+shares = (1, 2, 3, 4, 4, 4, 4, 4, 3, 2, 1)
+
+groups = (1, 2, 2, 2, 2, 2)
 
 
 def gelu_value(v):
@@ -20,7 +30,7 @@
     )
 
 
-def per_device(tokens, up_weight, hidden_grad):
+def plain_device(tokens, up_weight, hidden_grad):
     column_panel = lax.all_gather(up_weight, "row", axis=0, tiled=True)
     token_rows = lax.all_gather(tokens, "col", axis=1, tiled=True)
     preact = jnp.dot(token_rows, column_panel, preferred_element_type=jnp.float32)
@@ -38,9 +48,206 @@
     return (hidden, input_grad)
 
 
+def fill_panel(me, depth, kept_ref, got_ref, w_ref):
+    half = kept_ref.shape[0] // depth
+    bits = half.bit_length()
+    for source, base in ((kept_ref, 0), (got_ref, half)):
+
+        @pl.loop(0, half)
+        def _(j):
+            index = me
+            for step in range(bits):
+                index = index ^ ((((j + base) >> step) & 1) << (bits - 1 - step))
+            here = pl.ds(pl.multiple_of(index * depth, depth), depth)
+            w_ref[here, :] = source[pl.ds(pl.multiple_of(j * depth, depth), depth), :]
+
+
+def chunk_kernel(
+    depth, place, own, out_in, mid_in, cross, spread, kept_ref, got_ref, grad_ref, *rest
+):
+    hidden_ref, send_ref, keep_ref, w_ref = rest[-4:]
+
+    @pl.when(pl.program_id(0) == 0)
+    def _():
+        fill_panel(place[5], depth, kept_ref, got_ref, w_ref)
+
+    block = own.shape[1]
+    at = [pl.ds(pl.multiple_of(place[i] * block, block), block) for i in range(4)]
+    middle = place[4] == 1
+    partner = jnp.where(middle, out_in[...], mid_in[...])
+    far = jnp.where(middle, cross[...], spread[...])
+    v = jnp.dot(own[...], w_ref[at[0], :], preferred_element_type=jnp.float32)
+    v = v + jnp.dot(partner, w_ref[at[1], :], preferred_element_type=jnp.float32)
+    v = v + jnp.dot(far[:, :block], w_ref[at[2], :], preferred_element_type=jnp.float32)
+    v = v + jnp.dot(far[:, block:], w_ref[at[3], :], preferred_element_type=jnp.float32)
+    square = v * v
+    tval = jnp.tanh(gelu_c * (v + gelu_a * square * v))
+    gate = 0.5 * (1.0 + tval)
+    hidden_ref[...] = (v * gate).astype(hidden_ref.dtype)
+    slope = gate + 0.5 * v * (1.0 - tval * tval) * gelu_c * (1.0 + 3.0 * gelu_a * square)
+    pre_grad = (grad_ref[...].astype(jnp.float32) * slope).astype(jnp.bfloat16)
+
+    def term(i):
+        got = lax.dot_general(
+            pre_grad, w_ref[at[i], :], (((1,), (1,)), ((), ())), preferred_element_type=jnp.float32
+        )
+        return got.astype(jnp.bfloat16)
+
+    send_ref[:, :block] = term(2)
+    send_ref[:, block : 2 * block] = term(3)
+    send_ref[:, 2 * block :] = term(1)
+    keep_ref[...] = term(0)
+
+
+def chunk_call(place, tokens, out_in, mid_in, cross, spread, panel, grad, hidden, at, start):
+    size, block = cross.shape[0], tokens.shape[1]
+    rows, width = grad.shape
+    tile = 256 if size % 256 == 0 else size
+    first, in_group = at // tile, (at - start) // tile
+    depth, kept, got = panel
+    half = kept.shape[0]
+    features = 2 * half
+    args = [place, tokens, out_in, mid_in, cross, spread, kept, got, grad]
+    here = lambda i, p: (i, 0)
+    at_middle = lambda i, p: (i * p[4], 0)
+    at_outer = lambda i, p: (i * (1 - p[4]), 0)
+    all_rows = lambda i, p: (i + first, 0)
+    in_specs = [
+        pl.BlockSpec((tile, block), all_rows),
+        pl.BlockSpec((tile, block), lambda i, p: ((i + in_group) * p[4], 0)),
+        pl.BlockSpec((tile, block), lambda i, p: ((i + in_group) * (1 - p[4]), 0)),
+        pl.BlockSpec((tile, 2 * block), at_middle),
+        pl.BlockSpec((tile, 2 * block), at_outer),
+        pl.BlockSpec((half, width), lambda i, p: (0, 0)),
+        pl.BlockSpec((half, width), lambda i, p: (0, 0)),
+        pl.BlockSpec((tile, width), all_rows),
+    ]
+    aliases = {}
+    if hidden is not None:
+        aliases = {len(args): 0}
+        args.append(hidden)
+        in_specs.append(pl.BlockSpec(memory_space=pl.ANY))
+    return pl.pallas_call(
+        functools.partial(chunk_kernel, depth),
+        grid_spec=pltpu.PrefetchScalarGridSpec(
+            num_scalar_prefetch=1,
+            grid=(size // tile,),
+            in_specs=in_specs,
+            out_specs=[
+                pl.BlockSpec((tile, width), all_rows),
+                pl.BlockSpec((tile, 3 * block), here),
+                pl.BlockSpec((tile, block), here),
+            ],
+            scratch_shapes=[pltpu.VMEM((features, width), jnp.bfloat16)],
+        ),
+        out_shape=[
+            jax.ShapeDtypeStruct((rows, width), jnp.bfloat16),
+            jax.ShapeDtypeStruct((size, 3 * block), jnp.bfloat16),
+            jax.ShapeDtypeStruct((size, block), jnp.bfloat16),
+        ],
+        input_output_aliases=aliases,
+        compiler_params=pltpu.CompilerParams(vmem_limit_bytes=40 * 1024 * 1024),
+        cost_estimate=pl.CostEstimate(
+            flops=4 * size * features * width,
+            bytes_accessed=size * (16 * block + 4 * width) + 2 * features * width,
+            transcendentals=size * width,
+        ),
+    )(*args)
+
+
+def gather_panel(up_weight, n_row):
+    bits = n_row.bit_length() - 1
+    kept = up_weight
+    for step in range(bits):
+        bit = n_row >> (step + 1)
+        got = lax.ppermute(kept, "row", [(i, i ^ bit) for i in range(n_row)])
+        if step < bits - 1:
+            kept = jnp.concatenate([kept, got], axis=0)
+    return up_weight.shape[0], kept, got
+
+
+def line_device(n_row, tokens, up_weight, hidden_grad):
+    col = lax.axis_index("col").astype(jnp.int32)
+    inward = [(0, 1), (3, 2)]
+    outward = [(1, 0), (2, 3)]
+    across = [(1, 2), (2, 1)]
+
+    def send(x, pairs):
+        return lax.ppermute(x, "col", pairs)
+
+    rows, block = tokens.shape
+    unit = rows // sum(shares)
+    half = col // 2
+    is_middle = ((col == 1) | (col == 2)).astype(jnp.int32)
+    place = [col, col ^ 1, 2 - half, 3 * (1 - half), is_middle]
+    place = jnp.stack(place + [lax.axis_index("row").astype(jnp.int32)])
+
+    panel = gather_panel(up_weight, n_row)
+
+    grouped = []
+    at = 0
+    for index, count in enumerate(groups):
+        first = sum(groups[:index])
+        start, at = at, at + unit * sum(shares[first : first + count])
+        own = lax.slice_in_dim(tokens, start, at, axis=0)
+        pair = (send(own, inward), send(own, outward))
+        grouped += [(start,) + pair] * count
+
+    hidden = None
+    input_grad = jnp.zeros((rows, block), jnp.bfloat16)
+    at = 0
+    for index, share in enumerate(shares):
+        size = share * unit
+        start, out_in, mid_in = grouped[index]
+        own = lax.slice_in_dim(tokens, at, at + size, axis=0)
+        theirs = lax.slice_in_dim(out_in, at - start, at - start + size, axis=0)
+        both = jnp.concatenate([own, theirs], axis=1)
+        cross = send(both, across)
+        spread = send(cross, outward)
+        hidden, terms, keep = chunk_call(
+            place, tokens, out_in, mid_in, cross, spread, panel, hidden_grad, hidden, at, start
+        )
+        got = send(terms, inward)
+        far = terms[:, : 2 * block].astype(jnp.float32) + got[:, : 2 * block].astype(jnp.float32)
+        far = far.astype(jnp.bfloat16)
+        back = send(far, across)
+        theirs = terms[:, 2 * block :].astype(jnp.float32) + back[:, block:].astype(jnp.float32)
+        theirs = theirs.astype(jnp.bfloat16)
+        last = send(theirs, outward)
+        total = keep.astype(jnp.float32) + back[:, :block].astype(jnp.float32)
+        total = total + got[:, 2 * block :].astype(jnp.float32) + last.astype(jnp.float32)
+        input_grad = lax.dynamic_update_slice(input_grad, total.astype(jnp.bfloat16), (at, 0))
+        at += size
+    return (hidden, input_grad)
+
+
+def fits_line(mesh, tokens, up_weight):
+    n_row, n_col = mesh.shape["row"], mesh.shape["col"]
+    rows, block = tokens.shape[0] // n_row, tokens.shape[1] // n_col
+    return (
+        n_col == 4
+        and n_row > 1
+        and n_row & (n_row - 1) == 0
+        and rows % (16 * sum(shares)) == 0
+        and block % 128 == 0
+        and up_weight.shape[1] % (128 * n_col) == 0
+    )
+
+
 def solution(mesh):
-    in_specs = (P("row", "col"), P("row", "col"), P("row", "col"))
-    out_specs = (P("row", "col"), P("row", "col"))
-    return jax.shard_map(
-        per_device, mesh=mesh, in_specs=in_specs, out_specs=out_specs, check_vma=False
-    )
+    specs = (P("row", "col"), P("row", "col"), P("row", "col"))
+
+    def line_body(*blocks):
+        return line_device(mesh.shape["row"], *blocks)
+
+    def mapped(body):
+        return jax.shard_map(body, mesh=mesh, in_specs=specs, out_specs=specs[:2], check_vma=False)
+
+    ordered = mapped(line_body)
+
+    def whole(tokens, up_weight, hidden_grad):
+        if fits_line(mesh, tokens, up_weight):
+            return ordered(tokens, up_weight, hidden_grad)
+        return mapped(plain_device)(tokens, up_weight, hidden_grad)
+
+    return whole

time: 688 us -> 721 us (1.048)
  waiting for transfers between devices: 600 us -> 441 us
  starting transfers between devices: 0.11 us -> 142 us
  Pallas kernels: 0 us -> 86.1 us
  matrix products: 74.5 us -> 0 us
  local copies, waits for them, and re-layouts: 0.01 us -> 28.5 us
  other arithmetic: 0 us -> 19 us
  between operations: 13.7 us -> 2.12 us
    ppermute x0 -> x70, waiting for transfers between devices: none -> 441 us  [the longest x67 441 us: send(): return lax.ppermute(x, 'col', pairs)]
    all_gather x2 -> x0, waiting for transfers between devices: 320 us -> none  [the longest x1 288 us: per_device(): token_rows = lax.all_gather(tokens, 'col', axis=1, tiled=True)]
    reduce_scatter x1 -> x0, waiting for transfers between devices: 279 us -> none  [per_device(): lax.psum_scatter(lax.dot_general(column_panel, pre_grad, (((1,), (1,)), (...]
    ppermute x0 -> x70, starting transfers between devices: none -> 142 us  [the longest x67 139 us: send(): return lax.ppermute(x, 'col', pairs)]
    pallas_call x0 -> x11, Pallas kernels: none -> 86.1 us  [chunk_call(): pl.pallas_call(functools.partial(chunk_kernel, depth), grid_spec=pltpu.Pr...]
    dot_general x2 -> x0, matrix products: 74.5 us -> none  [the longest x1 40.1 us: per_device(): lax.dot_general(column_panel, pre_grad, (((1,), (1,)), ((), ())), preferr...]
    unnamed x2 -> x96, local copies, waits for them, and re-layouts: 0.01 us -> 12.5 us
    slice x0 -> x18, local copies, waits for them, and re-layouts: none -> 12.4 us  [the longest x4 5.41 us: line_device(): own = lax.slice_in_dim(tokens, start, at, axis=0)]
  transfers between devices with their start and end apart: 3 -> 70, of which waited for: 3 -> 28; matrix products, arithmetic and copies ran while one was open for 0% -> 5% of each run, Pallas kernels for 0% -> 12%
where the time goes in v2:
time: 721 us; the launch traced here: 718 us
  waiting for transfers between devices  441 us (61%)
  starting transfers between devices  142 us (20%)
  Pallas kernels  86.1 us (12%)
  local copies, waits for them, and re-layouts  28.5 us (4%)
  other arithmetic  19 us (3%)
    ppermute x67, waiting for transfers between devices, send(): return lax.ppermute(x, 'col', pairs)  441 us
    ppermute x67, starting transfers between devices, send(): return lax.ppermute(x, 'col', pairs)  139 us
    pallas_call x11, Pallas kernels, chunk_call(): pl.pallas_call(functools.partial(chunk_kernel, depth), grid_spec=pltpu.Pr...  86.1 us
  transfers between devices with their start and end apart: 70, of which 28 were waited for; matrix products, arithmetic and copies ran while one was open for 5% of the time, Pallas kernels for 12%

profile of v2, /device:TPU:0, one launch (start us, length us, event | category | flops | bytes accessed | tf_op | source)
XLA Modules:
  0.0 718.2 jit_solution(7720898732362095589)
XLA Ops:
  65.0 17.2 %collective-permute-done.9.out_in = bf16[1792,256]{1,0:T(8,128)(2,1)} collective-permute-done((bf16[1792,256]{1,0:T(8,128)(2,1)}, bf16[1792,256]{1,0:T(8,128)(2,1)}, u32[]{:S(2)}, u32[]{:S(2)}) %collective-permute-start.9) | collective-permute-done | bytes 917536 | tf_op jit(solution)/shard_map/ppermute | solution.py:176
  84.0 18.8 %collective-permute-done.15.out_in = bf16[2048,256]{1,0:T(8,128)(2,1)S(1)} collective-permute-done((bf16[2048,256]{1,0:T(8,128)(2,1)}, bf16[2048,256]{1,0:T(8,128)(2,1)S(1)}, u32[]{:S(2)}, u32[]{:S(2)}) %collective-permute-start.15) | collective-permute-done | bytes 1048608 | tf_op jit(solution)/shard_map/ppermute | solution.py:176
  135.4 30.6 %collective-permute-start.40 = (bf16[512,768]{1,0:T(8,128)(2,1)S(1)}, bf16[512,768]{1,0:T(8,128)(2,1)}, u32[]{:S(2)}, u32[]{:S(2)}) collective-permute-start(bf16[512,768]{1,0:T(8,128)(2,1)S(1)} %get-tuple-element.49), channel_id=1, source_target_pairs={{0,1},{3,2},{4,5},{7,6},{8,9},{11,10},{12,13},{15,14},{16,17},{19,... | collective-permute-start | bytes 2359304 | tf_op jit(solution)/shard_map/ppermute | solution.py:176
  173.5 63.6 %collective-permute-done.39 = bf16[256,256]{1,0:T(8,128)(2,1)S(1)} collective-permute-done((bf16[256,256]{1,0:T(8,128)(2,1)S(1)}, bf16[256,256]{1,0:T(8,128)(2,1)S(1)}, u32[]{:S(2)}, u32[]{:S(2)}) %collective-permute-start.39) | collective-permute-done | bytes 131104 | tf_op jit(solution)/shard_map/ppermute | solution.py:176
  258.1 9.8 %shard_map.53 = (bf16[8192,1024]{1,0:T(8,128)(2,1)}, bf16[1024,768]{1,0:T(8,128)(2,1)S(1)}, bf16[1024,256]{1,0:T(8,128)(2,1)S(1)}) custom-call(s32[6]{0:T(128)S(1)} %stack.31.place, bf16[8192,256]{1,0:T(8,128)(2,1)S(1)} %copy-done.1, bf16[2048,256]{1,0:T(8,128)(2,1)S(1)} %collective-permute-done.21.out_in, ...), custom_call_target="tpu_custom_call", output_to_operand_aliasing={{0}: (9, {})} | custom-call | flops 4294967296 | bytes 10485760 | tf_op jit(solution)/shard_map/pallas_call | solution.py:130
  271.6 10.5 %collective-permute-done.24.spread = bf16[1024,512]{1,0:T(8,128)(2,1)} collective-permute-done((bf16[1024,512]{1,0:T(8,128)(2,1)S(1)}, bf16[1024,512]{1,0:T(8,128)(2,1)}, u32[]{:S(2)}, u32[]{:S(2)}) %collective-permute-start.24) | collective-permute-done | bytes 1048608 | tf_op jit(solution)/shard_map/ppermute | solution.py:176
  283.4 9.9 %shard_map.54 = (bf16[8192,1024]{1,0:T(8,128)(2,1)}, bf16[1024,768]{1,0:T(8,128)(2,1)S(1)}, bf16[1024,256]{1,0:T(8,128)(2,1)S(1)}) custom-call(s32[6]{0:T(128)S(1)} %stack.31.place, bf16[8192,256]{1,0:T(8,128)(2,1)S(1)} %copy-done.1, bf16[2048,256]{1,0:T(8,128)(2,1)S(1)} %collective-permute-done.21.out_in, ...), custom_call_target="tpu_custom_call", output_to_operand_aliasing={{0}: (9, {})} | custom-call | flops 4294967296 | bytes 10485760 | tf_op jit(solution)/shard_map/pallas_call | solution.py:130
  293.3 11.1 %collective-permute-done.20.spread = bf16[1024,512]{1,0:T(8,128)(2,1)S(1)} collective-permute-done((bf16[1024,512]{1,0:T(8,128)(2,1)S(1)}, bf16[1024,512]{1,0:T(8,128)(2,1)S(1)}, u32[]{:S(2)}, u32[]{:S(2)}) %collective-permute-start.20) | collective-permute-done | bytes 1048608 | tf_op jit(solution)/shard_map/ppermute | solution.py:176
  305.9 9.8 %shard_map.55 = (bf16[8192,1024]{1,0:T(8,128)(2,1)}, bf16[1024,768]{1,0:T(8,128)(2,1)S(1)}, bf16[1024,256]{1,0:T(8,128)(2,1)S(1)}) custom-call(s32[6]{0:T(128)S(1)} %stack.31.place, bf16[8192,256]{1,0:T(8,128)(2,1)S(1)} %copy-done.1, bf16[2048,256]{1,0:T(8,128)(2,1)S(1)} %collective-permute-done.15.out_in, ...), custom_call_target="tpu_custom_call", output_to_operand_aliasing={{0}: (9, {})} | custom-call | flops 4294967296 | bytes 10485760 | tf_op jit(solution)/shard_map/pallas_call | solution.py:130
  317.8 9.1 %collective-permute-done.18.spread = bf16[1024,512]{1,0:T(8,128)(2,1)S(1)} collective-permute-done((bf16[1024,512]{1,0:T(8,128)(2,1)S(1)}, bf16[1024,512]{1,0:T(8,128)(2,1)S(1)}, u32[]{:S(2)}, u32[]{:S(2)}) %collective-permute-start.18) | collective-permute-done | bytes 1048608 | tf_op jit(solution)/shard_map/ppermute | solution.py:176
  329.4 9.8 %shard_map.56 = (bf16[8192,1024]{1,0:T(8,128)(2,1)}, bf16[1024,768]{1,0:T(8,128)(2,1)S(1)}, bf16[1024,256]{1,0:T(8,128)(2,1)S(1)}) custom-call(s32[6]{0:T(128)S(1)} %stack.31.place, bf16[8192,256]{1,0:T(8,128)(2,1)S(1)} %copy-done.1, bf16[2048,256]{1,0:T(8,128)(2,1)S(1)} %collective-permute-done.15.out_in, ...), custom_call_target="tpu_custom_call", output_to_operand_aliasing={{0}: (9, {})} | custom-call | flops 4294967296 | bytes 10485760 | tf_op jit(solution)/shard_map/pallas_call | solution.py:130
  349.2 19.9 %collective-permute-done.14.spread = bf16[1024,512]{1,0:T(8,128)(2,1)S(1)} collective-permute-done((bf16[1024,512]{1,0:T(8,128)(2,1)}, bf16[1024,512]{1,0:T(8,128)(2,1)S(1)}, u32[]{:S(2)}, u32[]{:S(2)}) %collective-permute-start.14) | collective-permute-done | bytes 1048608 | tf_op jit(solution)/shard_map/ppermute | solution.py:176
  370.3 10.0 %shard_map.57 = (bf16[8192,1024]{1,0:T(8,128)(2,1)}, bf16[1024,768]{1,0:T(8,128)(2,1)S(1)}, bf16[1024,256]{1,0:T(8,128)(2,1)S(1)}) custom-call(s32[6]{0:T(128)S(1)} %stack.31.place, bf16[8192,256]{1,0:T(8,128)(2,1)S(1)} %copy-done.1, bf16[1792,256]{1,0:T(8,128)(2,1)} %collective-permute-done.9.out_in, ...), custom_call_target="tpu_custom_call", output_to_operand_aliasing={{0}: (9, {})} | custom-call | flops 4294967296 | bytes 10485760 | tf_op jit(solution)/shard_map/pallas_call | solution.py:130
  396.9 8.9 %collective-permute-done.8.spread = bf16[512,512]{1,0:T(8,128)(2,1)S(1)} collective-permute-done((bf16[512,512]{1,0:T(8,128)(2,1)}, bf16[512,512]{1,0:T(8,128)(2,1)S(1)}, u32[]{:S(2)}, u32[]{:S(2)}) %collective-permute-start.8) | collective-permute-done | bytes 524320 | tf_op jit(solution)/shard_map/ppermute | solution.py:176
  425.2 14.7 %collective-permute-done.67 = bf16[256,768]{1,0:T(8,128)(2,1)S(1)} collective-permute-done((bf16[256,768]{1,0:T(8,128)(2,1)S(1)}, bf16[256,768]{1,0:T(8,128)(2,1)S(1)}, u32[]{:S(2)}, u32[]{:S(2)}) %collective-permute-start.67) | collective-permute-done | bytes 393248 | tf_op jit(solution)/shard_map/ppermute | solution.py:176
  477.6 21.2 %collective-permute-done.58 = bf16[1024,768]{1,0:T(8,128)(2,1)S(1)} collective-permute-done((bf16[1024,768]{1,0:T(8,128)(2,1)S(1)}, bf16[1024,768]{1,0:T(8,128)(2,1)S(1)}, u32[]{:S(2)}, u32[]{:S(2)}) %collective-permute-start.58) | collective-permute-done | bytes 1572896 | tf_op jit(solution)/shard_map/ppermute | solution.py:176
  499.8 32.7 %collective-permute-done.55 = bf16[1024,768]{1,0:T(8,128)(2,1)S(1)} collective-permute-done((bf16[1024,768]{1,0:T(8,128)(2,1)S(1)}, bf16[1024,768]{1,0:T(8,128)(2,1)S(1)}, u32[]{:S(2)}, u32[]{:S(2)}) %collective-permute-start.55) | collective-permute-done | bytes 1572896 | tf_op jit(solution)/shard_map/ppermute | solution.py:176
  533.6 32.7 %collective-permute-done.49 = bf16[1024,768]{1,0:T(8,128)(2,1)S(1)} collective-permute-done((bf16[1024,768]{1,0:T(8,128)(2,1)S(1)}, bf16[1024,768]{1,0:T(8,128)(2,1)S(1)}, u32[]{:S(2)}, u32[]{:S(2)}) %collective-permute-start.49) | collective-permute-done | bytes 1572896 | tf_op jit(solution)/shard_map/ppermute | solution.py:176
  567.3 32.7 %collective-permute-done.46 = bf16[1024,768]{1,0:T(8,128)(2,1)S(1)} collective-permute-done((bf16[1024,768]{1,0:T(8,128)(2,1)S(1)}, bf16[1024,768]{1,0:T(8,128)(2,1)S(1)}, u32[]{:S(2)}, u32[]{:S(2)}) %collective-permute-start.46) | collective-permute-done | bytes 1572896 | tf_op jit(solution)/shard_map/ppermute | solution.py:176
  601.0 26.4 %collective-permute-done.52 = bf16[1024,768]{1,0:T(8,128)(2,1)S(1)} collective-permute-done((bf16[1024,768]{1,0:T(8,128)(2,1)S(1)}, bf16[1024,768]{1,0:T(8,128)(2,1)S(1)}, u32[]{:S(2)}, u32[]{:S(2)}) %collective-permute-start.52) | collective-permute-done | bytes 1572896 | tf_op jit(solution)/shard_map/ppermute | solution.py:176
  637.2 35.4 %collective-permute-done.48 = bf16[1024,256]{1,0:T(8,128)(2,1)S(1)} collective-permute-done((bf16[1024,256]{1,0:T(8,128)(2,1)S(1)}, bf16[1024,256]{1,0:T(8,128)(2,1)S(1)}, u32[]{:S(2)}, u32[]{:S(2)}) %collective-permute-start.48) | collective-permute-done | bytes 524320 | tf_op jit(solution)/shard_map/ppermute | solution.py:176
  674.2 13.1 %collective-permute-done.51 = bf16[1024,256]{1,0:T(8,128)(2,1)S(1)} collective-permute-done((bf16[1024,256]{1,0:T(8,128)(2,1)S(1)}, bf16[1024,256]{1,0:T(8,128)(2,1)S(1)}, u32[]{:S(2)}, u32[]{:S(2)}) %collective-permute-start.51) | collective-permute-done | bytes 524320 | tf_op jit(solution)/shard_map/ppermute | solution.py:176
  688.8 9.7 %collective-permute-done.54 = bf16[1024,256]{1,0:T(8,128)(2,1)S(1)} collective-permute-done((bf16[1024,256]{1,0:T(8,128)(2,1)S(1)}, bf16[1024,256]{1,0:T(8,128)(2,1)S(1)}, u32[]{:S(2)}, u32[]{:S(2)}) %collective-permute-start.54) | collective-permute-done | bytes 524320 | tf_op jit(solution)/shard_map/ppermute | solution.py:176
  700.1 9.6 %collective-permute-done.57 = bf16[1024,256]{1,0:T(8,128)(2,1)S(1)} collective-permute-done((bf16[1024,256]{1,0:T(8,128)(2,1)S(1)}, bf16[1024,256]{1,0:T(8,128)(2,1)S(1)}, u32[]{:S(2)}, u32[]{:S(2)}) %collective-permute-start.57) | collective-permute-done | bytes 524320 | tf_op jit(solution)/shard_map/ppermute | solution.py:176
  (289 shorter events, 248.9 us)
Async XLA Ops:
  23.3 59.7 %collective-permute-start.21 = (bf16[2048,256]{1,0:T(8,128)(2,1)}, bf16[2048,256]{1,0:T(8,128)(2,1)S(1)}, u32[]{:S(2)}, u32[]{:S(2)}) collective-permute-start(bf16[2048,256]{1,0:T(8,128)(2,1)} %get-tuple-element.80), channel_id=1, source_target_pairs={{0,1},{3,2},{4,5},{7,6},{8,9},{11,10},{12,13},{15,14},{16,17},{19,... | collective-permute-start | bytes 3145736 | tf_op jit(solution)/shard_map/ppermute | solution.py:176
  28.1 54.1 %collective-permute-start.9 = (bf16[1792,256]{1,0:T(8,128)(2,1)}, bf16[1792,256]{1,0:T(8,128)(2,1)}, u32[]{:S(2)}, u32[]{:S(2)}) collective-permute-start(bf16[1792,256]{1,0:T(8,128)(2,1)} %slice.282), channel_id=1, source_target_pairs={{0,1},{3,2},{4,5},{7,6},{8,9},{11,10},{12,13},{15,14},{16,17},{19,... | collective-permute-start | bytes 2752520 | tf_op jit(solution)/shard_map/ppermute | solution.py:176
  135.4 115.6 %collective-permute-start.40 = (bf16[512,768]{1,0:T(8,128)(2,1)S(1)}, bf16[512,768]{1,0:T(8,128)(2,1)}, u32[]{:S(2)}, u32[]{:S(2)}) collective-permute-start(bf16[512,768]{1,0:T(8,128)(2,1)S(1)} %get-tuple-element.49), channel_id=1, source_target_pairs={{0,1},{3,2},{4,5},{7,6},{8,9},{11,10},{12,13},{15,14},{16,17},{19,... | collective-permute-start | bytes 2359304 | tf_op jit(solution)/shard_map/ppermute | solution.py:176
  166.0 88.3 %collective-permute-start.26 = (bf16[1024,512]{1,0:T(8,128)(2,1)S(1)}, bf16[1024,512]{1,0:T(8,128)(2,1)S(1)}, u32[]{:S(2)}, u32[]{:S(2)}) collective-permute-start(bf16[1024,512]{1,0:T(8,128)(2,1)S(1)} %collective-permute-done.25.cross), channel_id=1, source_target_pairs={{1,0},{2,3},{5,4},{6,7},{9,8},{10,11},{13,12},{14,15},{17,16},{18,... | collective-permute-start | bytes 3145736 | tf_op jit(solution)/shard_map/ppermute | solution.py:176
  167.3 69.7 %collective-permute-start.39 = (bf16[256,256]{1,0:T(8,128)(2,1)S(1)}, bf16[256,256]{1,0:T(8,128)(2,1)S(1)}, u32[]{:S(2)}, u32[]{:S(2)}) collective-permute-start(bf16[256,256]{1,0:T(8,128)(2,1)S(1)} %add_convert_fusion.32), channel_id=1, source_target_pairs={{1,0},{2,3},{5,4},{6,7},{9,8},{10,11},{13,12},{14,15},{17,16},{18,... | collective-permute-start | bytes 393224 | tf_op jit(solution)/shard_map/ppermute | solution.py:176
  169.6 99.1 %collective-permute-start.16 = (bf16[2048,256]{1,0:T(8,128)(2,1)}, bf16[2048,256]{1,0:T(8,128)(2,1)S(1)}, u32[]{:S(2)}, u32[]{:S(2)}) collective-permute-start(bf16[2048,256]{1,0:T(8,128)(2,1)} %get-tuple-element.81), channel_id=1, source_target_pairs={{1,0},{2,3},{5,4},{6,7},{9,8},{10,11},{13,12},{14,15},{17,16},{18,... | collective-permute-start | bytes 3145736 | tf_op jit(solution)/shard_map/ppermute | solution.py:176
  171.8 98.2 %collective-permute-start.13 = (bf16[1024,512]{1,0:T(8,128)(2,1)}, bf16[1024,512]{1,0:T(8,128)(2,1)}, u32[]{:S(2)}, u32[]{:S(2)}) collective-permute-start(bf16[1024,512]{1,0:T(8,128)(2,1)} %pad_maximum_fusion), channel_id=1, source_target_pairs={{1,2},{2,1},{5,6},{6,5},{9,10},{10,9},{13,14},{14,13},{17,18},{18,... | collective-permute-start | bytes 3145736 | tf_op jit(solution)/shard_map/ppermute | solution.py:176
  255.4 71.5 %collective-permute-start.18 = (bf16[1024,512]{1,0:T(8,128)(2,1)S(1)}, bf16[1024,512]{1,0:T(8,128)(2,1)S(1)}, u32[]{:S(2)}, u32[]{:S(2)}) collective-permute-start(bf16[1024,512]{1,0:T(8,128)(2,1)S(1)} %collective-permute-done.17.cross), channel_id=1, source_target_pairs={{1,0},{2,3},{5,4},{6,7},{9,8},{10,11},{13,12},{14,15},{17,16},{18,... | collective-permute-start | bytes 3145736 | tf_op jit(solution)/shard_map/ppermute | solution.py:176
  268.7 77.9 %collective-permute-start.10 = (bf16[1792,256]{1,0:T(8,128)(2,1)}, bf16[1792,256]{1,0:T(8,128)(2,1)S(1)}, u32[]{:S(2)}, u32[]{:S(2)}) collective-permute-start(bf16[1792,256]{1,0:T(8,128)(2,1)} %slice.282), channel_id=1, source_target_pairs={{1,0},{2,3},{5,4},{6,7},{9,8},{10,11},{13,12},{14,15},{17,16},{18,... | collective-permute-start | bytes 2752520 | tf_op jit(solution)/shard_map/ppermute | solution.py:176
  282.1 87.0 %collective-permute-start.14 = (bf16[1024,512]{1,0:T(8,128)(2,1)}, bf16[1024,512]{1,0:T(8,128)(2,1)S(1)}, u32[]{:S(2)}, u32[]{:S(2)}) collective-permute-start(bf16[1024,512]{1,0:T(8,128)(2,1)} %collective-permute-done.13.cross), channel_id=1, source_target_pairs={{1,0},{2,3},{5,4},{6,7},{9,8},{10,11},{13,12},{14,15},{17,16},{18,... | collective-permute-start | bytes 3145736 | tf_op jit(solution)/shard_map/ppermute | solution.py:176
  316.5 69.4 %collective-permute-start.12 = (bf16[768,512]{1,0:T(8,128)(2,1)}, bf16[768,512]{1,0:T(8,128)(2,1)S(1)}, u32[]{:S(2)}, u32[]{:S(2)}) collective-permute-start(bf16[768,512]{1,0:T(8,128)(2,1)} %collective-permute-done.11.cross), channel_id=1, source_target_pairs={{1,0},{2,3},{5,4},{6,7},{9,8},{10,11},{13,12},{14,15},{17,16},{18,... | collective-permute-start | bytes 2359304 | tf_op jit(solution)/shard_map/ppermute | solution.py:176
  326.9 93.2 %collective-permute-start.43 = (bf16[768,768]{1,0:T(8,128)(2,1)}, bf16[768,768]{1,0:T(8,128)(2,1)}, u32[]{:S(2)}, u32[]{:S(2)}) collective-permute-start(bf16[768,768]{1,0:T(8,128)(2,1)} %get-tuple-element.51), channel_id=1, source_target_pairs={{0,1},{3,2},{4,5},{7,6},{8,9},{11,10},{12,13},{15,14},{16,17},{19,... | collective-permute-start | bytes 3538952 | tf_op jit(solution)/shard_map/ppermute | solution.py:176
  347.9 65.7 %collective-permute-start.3 = (bf16[256,512]{1,0:T(8,128)(2,1)}, bf16[256,512]{1,0:T(8,128)(2,1)S(1)}, u32[]{:S(2)}, u32[]{:S(2)}) collective-permute-start(bf16[256,512]{1,0:T(8,128)(2,1)} %collective-permute-done.2.cross), channel_id=1, source_target_pairs={{1,0},{2,3},{5,4},{6,7},{9,8},{10,11},{13,12},{14,15},{17,16},{18,... | collective-permute-start | bytes 786440 | tf_op jit(solution)/shard_map/ppermute | solution.py:176
  420.2 78.7 %collective-permute-start.58 = (bf16[1024,768]{1,0:T(8,128)(2,1)S(1)}, bf16[1024,768]{1,0:T(8,128)(2,1)S(1)}, u32[]{:S(2)}, u32[]{:S(2)}) collective-permute-start(bf16[1024,768]{1,0:T(8,128)(2,1)S(1)} %get-tuple-element.61), channel_id=1, source_target_pairs={{0,1},{3,2},{4,5},{7,6},{8,9},{11,10},{12,13},{15,14},{16,17},{19,... | collective-permute-start | bytes 4718600 | tf_op jit(solution)/shard_map/ppermute | solution.py:176
  449.9 82.6 %collective-permute-start.55 = (bf16[1024,768]{1,0:T(8,128)(2,1)S(1)}, bf16[1024,768]{1,0:T(8,128)(2,1)S(1)}, u32[]{:S(2)}, u32[]{:S(2)}) collective-permute-start(bf16[1024,768]{1,0:T(8,128)(2,1)S(1)} %get-tuple-element.59), channel_id=1, source_target_pairs={{0,1},{3,2},{4,5},{7,6},{8,9},{11,10},{12,13},{15,14},{16,17},{19,... | collective-permute-start | bytes 4718600 | tf_op jit(solution)/shard_map/ppermute | solution.py:176
  455.4 110.9 %collective-permute-start.49 = (bf16[1024,768]{1,0:T(8,128)(2,1)S(1)}, bf16[1024,768]{1,0:T(8,128)(2,1)S(1)}, u32[]{:S(2)}, u32[]{:S(2)}) collective-permute-start(bf16[1024,768]{1,0:T(8,128)(2,1)S(1)} %get-tuple-element.55), channel_id=1, source_target_pairs={{0,1},{3,2},{4,5},{7,6},{8,9},{11,10},{12,13},{15,14},{16,17},{19,... | collective-permute-start | bytes 4718600 | tf_op jit(solution)/shard_map/ppermute | solution.py:176
  466.5 133.5 %collective-permute-start.46 = (bf16[1024,768]{1,0:T(8,128)(2,1)S(1)}, bf16[1024,768]{1,0:T(8,128)(2,1)S(1)}, u32[]{:S(2)}, u32[]{:S(2)}) collective-permute-start(bf16[1024,768]{1,0:T(8,128)(2,1)S(1)} %get-tuple-element.53), channel_id=1, source_target_pairs={{0,1},{3,2},{4,5},{7,6},{8,9},{11,10},{12,13},{15,14},{16,17},{19,... | collective-permute-start | bytes 4718600 | tf_op jit(solution)/shard_map/ppermute | solution.py:176
  474.8 152.6 %collective-permute-start.52 = (bf16[1024,768]{1,0:T(8,128)(2,1)S(1)}, bf16[1024,768]{1,0:T(8,128)(2,1)S(1)}, u32[]{:S(2)}, u32[]{:S(2)}) collective-permute-start(bf16[1024,768]{1,0:T(8,128)(2,1)S(1)} %get-tuple-element.57), channel_id=1, source_target_pairs={{0,1},{3,2},{4,5},{7,6},{8,9},{11,10},{12,13},{15,14},{16,17},{19,... | collective-permute-start | bytes 4718600 | tf_op jit(solution)/shard_map/ppermute | solution.py:176
  498.9 129.7 %collective-permute-start.62 = (bf16[768,512]{1,0:T(8,128)(2,1)S(1)}, bf16[768,512]{1,0:T(8,128)(2,1)S(1)}, u32[]{:S(2)}, u32[]{:S(2)}) collective-permute-start(bf16[768,512]{1,0:T(8,128)(2,1)S(1)} %add_convert_fusion.5), channel_id=1, source_target_pairs={{1,2},{2,1},{5,6},{6,5},{9,10},{10,9},{13,14},{14,13},{17,18},{18,... | collective-permute-start | bytes 2359304 | tf_op jit(solution)/shard_map/ppermute | solution.py:176
  532.6 97.4 %collective-permute-start.59 = (bf16[1024,512]{1,0:T(8,128)(2,1)S(1)}, bf16[1024,512]{1,0:T(8,128)(2,1)S(1)}, u32[]{:S(2)}, u32[]{:S(2)}) collective-permute-start(bf16[1024,512]{1,0:T(8,128)(2,1)S(1)} %add_convert_fusion), channel_id=1, source_target_pairs={{1,2},{2,1},{5,6},{6,5},{9,10},{10,9},{13,14},{14,13},{17,18},{18,... | collective-permute-start | bytes 3145736 | tf_op jit(solution)/shard_map/ppermute | solution.py:176
  566.3 64.6 %collective-permute-start.56 = (bf16[1024,512]{1,0:T(8,128)(2,1)S(1)}, bf16[1024,512]{1,0:T(8,128)(2,1)S(1)}, u32[]{:S(2)}, u32[]{:S(2)}) collective-permute-start(bf16[1024,512]{1,0:T(8,128)(2,1)S(1)} %add_convert_fusion.1), channel_id=1, source_target_pairs={{1,2},{2,1},{5,6},{6,5},{9,10},{10,9},{13,14},{14,13},{17,18},{18,... | collective-permute-start | bytes 3145736 | tf_op jit(solution)/shard_map/ppermute | solution.py:176
  628.5 87.6 %collective-permute-start.69 = (bf16[256,256]{1,0:T(8,128)(2,1)S(1)}, bf16[256,256]{1,0:T(8,128)(2,1)S(1)}, u32[]{:S(2)}, u32[]{:S(2)}) collective-permute-start(bf16[256,256]{1,0:T(8,128)(2,1)S(1)} %add_convert_fusion.30), channel_id=1, source_target_pairs={{1,0},{2,3},{5,4},{6,7},{9,8},{10,11},{13,12},{14,15},{17,16},{18,... | collective-permute-start | bytes 393224 | tf_op jit(solution)/shard_map/ppermute | solution.py:176
  630.8 85.1 %collective-permute-start.66 = (bf16[512,256]{1,0:T(8,128)(2,1)S(1)}, bf16[512,256]{1,0:T(8,128)(2,1)S(1)}, u32[]{:S(2)}, u32[]{:S(2)}) collective-permute-start(bf16[512,256]{1,0:T(8,128)(2,1)S(1)} %add_convert_fusion.25), channel_id=1, source_target_pairs={{1,0},{2,3},{5,4},{6,7},{9,8},{10,11},{13,12},{14,15},{17,16},{18,... | collective-permute-start | bytes 786440 | tf_op jit(solution)/shard_map/ppermute | solution.py:176
  632.3 83.4 %collective-permute-start.63 = (bf16[768,256]{1,0:T(8,128)(2,1)S(1)}, bf16[768,256]{1,0:T(8,128)(2,1)S(1)}, u32[]{:S(2)}, u32[]{:S(2)}) collective-permute-start(bf16[768,256]{1,0:T(8,128)(2,1)S(1)} %add_convert_fusion.20), channel_id=1, source_target_pairs={{1,0},{2,3},{5,4},{6,7},{9,8},{10,11},{13,12},{14,15},{17,16},{18,... | collective-permute-start | bytes 1179656 | tf_op jit(solution)/shard_map/ppermute | solution.py:176
  (96 other events, 2271.0 us)
